TPU v7x, 512 devices: a whole 4x4x16 slice. The times are simulated.
512 devices in a mesh: dp: 32 (over z, x_hi), lon: 16 (over y, x_lo, core).
Axes of the slice: x: 4 (x_hi: 2, x_lo: 2; x = x_hi * 2 + x_lo), y: 4, z: 16, core: 2. Of those that a mesh axis runs over, the one named last changes fastest.
Arguments:
- fields: bfloat16 [32, 128, 48, 768], P('dp', 'lon'), may hold values from -6 to 6
- cotangent: bfloat16 [32, 128, 48, 768], P('dp', 'lon'), may hold values from -6 to 6
- first_weight: bfloat16 [2, 8, 96, 96], replicated, may hold values from -0.4375 to 0.4375
- second_weight: bfloat16 [2, 8, 96, 96], replicated, may hold values from -0.4375 to 0.4375
Outputs:
- layer_out: bfloat16 [32, 128, 48, 768], P('dp', 'lon')
- field_grad: bfloat16 [32, 128, 48, 768], P('dp', 'lon')
- first_grad: float32 [2, 8, 96, 96], replicated
- second_grad: float32 [2, 8, 96, 96], replicated
All inputs are finite; a program needn't handle non-finite values.
Results may differ from a plain program's by a relative error of at most 0.015.
Values may be sent and summed in bfloat16 or wider, within the bound.
A program may use at most 64 MiB of HBM per device.

v0:
```python
import math
import jax
import jax.numpy as jnp
from jax import lax
from jax.sharding import PartitionSpec as P

COEF = 0.7978845608028654
CUBIC = 0.044715


def gelu_value(inner):
    hyper = jnp.tanh(COEF * (inner + CUBIC * inner * inner * inner))
    return 0.5 * inner * (1.0 + hyper)


def gelu_slope(inner):
    hyper = jnp.tanh(COEF * (inner + CUBIC * inner * inner * inner))
    return 0.5 * (1.0 + hyper) + 0.5 * inner * (1.0 - hyper * hyper) * COEF * (
        1.0 + 3.0 * CUBIC * inner * inner
    )


def make_basis(length, count):
    cell_idx = jnp.arange(length, dtype=jnp.int32)
    mode_idx = jnp.arange(count, dtype=jnp.int32)
    product = cell_idx[:, None] * mode_idx[None, :] % length
    angle = product.astype(jnp.float32) * jnp.float32(2.0 * math.pi / length)
    return jnp.stack([jnp.cos(angle), -jnp.sin(angle)], axis=-1).astype(jnp.bfloat16)


def lat_apply(spec, table, lat_scale):
    return (
        jnp.einsum("kphc,phqj->kqjc", spec, table, preferred_element_type=jnp.float32) * lat_scale
    ).astype(jnp.bfloat16)


def forward_weight(weight):
    return jnp.stack([jnp.stack([weight[0], weight[1]]), jnp.stack([-weight[1], weight[0]])])


def adjoint_weight(weight):
    return jnp.stack([jnp.stack([weight[0], -weight[1]]), jnp.stack([weight[1], weight[0]])])


def block_product(spec, stacked):
    return jnp.einsum("kphbi,pqbij->kqhbj", spec, stacked, preferred_element_type=jnp.float32)


def block_adjoint(spec, stacked):
    return jnp.einsum("kphbj,pqbij->kqhbi", spec, stacked, preferred_element_type=jnp.float32)


def block_outer(left, right):
    pairs = jnp.einsum("kphbi,kqhbj->pqbij", left, right, preferred_element_type=jnp.float32)
    return jnp.stack([pairs[0, 0] + pairs[1, 1], pairs[0, 1] - pairs[1, 0]])


def on_device(fields, cotangent, first_weight, second_weight):
    cell_rows = fields[0]
    cot_rows = cotangent[0]
    lat_rows = cell_rows.shape[1]
    channels = cell_rows.shape[2]
    groups = first_weight.shape[1]
    group_width = first_weight.shape[2]
    lon_count = lax.axis_size("lon")
    total_cells = cell_rows.shape[0] * lon_count
    dft_basis = make_basis(total_cells, total_cells // 2)
    lat_basis = make_basis(lat_rows, lat_rows)
    cos_tab = lat_basis[:, :, 0]
    sin_tab = lat_basis[:, :, 1]
    lat_fwd_table = jnp.stack(
        [jnp.stack([cos_tab, sin_tab], axis=1), jnp.stack([-sin_tab, cos_tab], axis=1)], axis=0
    )
    lat_inv_table = jnp.stack(
        [jnp.stack([cos_tab.T, -sin_tab.T], axis=1), jnp.stack([sin_tab.T, cos_tab.T], axis=1)],
        axis=0,
    )
    norm_scale = 1.0 / math.sqrt(total_cells)
    lat_scale = 1.0 / math.sqrt(lat_rows)
    local_modes = cell_rows.shape[0] // 2
    mode_idx = lax.axis_index("lon") * local_modes + jnp.arange(local_modes, dtype=jnp.int32)
    mode_weight = jnp.where(mode_idx == 0, 1.0, 2.0).astype(jnp.bfloat16)[:, None, None, None]
    first_fwd = forward_weight(first_weight)
    second_fwd = forward_weight(second_weight)
    first_adj = adjoint_weight(first_weight)
    second_adj = adjoint_weight(second_weight)

    def local_dft(all_lines):
        return (
            jnp.einsum("whc,wkp->kphc", all_lines, dft_basis, preferred_element_type=jnp.float32)
            * norm_scale
        ).astype(jnp.bfloat16)

    def local_idft(all_modes):
        return (
            jnp.einsum("kphc,wkp->whc", all_modes, dft_basis, preferred_element_type=jnp.float32)
            * norm_scale
        ).astype(jnp.bfloat16)

    def lines_to_modes(all_lines):
        return lax.all_to_all(local_dft(all_lines), "lon", split_axis=0, concat_axis=3, tiled=True)

    def modes_to_lines(all_modes):
        return lax.all_to_all(local_idft(all_modes), "lon", split_axis=0, concat_axis=2, tiled=True)

    def to_spectrum(grid_rows):
        return lines_to_modes(
            lax.all_to_all(grid_rows, "lon", split_axis=2, concat_axis=0, tiled=True)
        )

    def to_cells(spec_rows):
        return modes_to_lines(
            lax.all_to_all(spec_rows, "lon", split_axis=3, concat_axis=0, tiled=True)
        )

    def split_groups(spec_rows):
        return spec_rows.reshape(local_modes, 2, lat_rows, groups, group_width)

    def join_groups(spec_rows):
        return spec_rows.astype(jnp.bfloat16).reshape(local_modes, 2, lat_rows, channels)

    lon_spec = to_spectrum(cell_rows)
    spectrum = split_groups(lat_apply(lon_spec, lat_fwd_table, lat_scale))
    inner = block_product(spectrum, first_fwd)
    act = gelu_value(inner).astype(jnp.bfloat16)
    mixed = join_groups(block_product(act, second_fwd)) * mode_weight
    mixed_lon = lat_apply(mixed, lat_inv_table, lat_scale)
    wave = to_cells(mixed_lon)
    dual_lon = to_spectrum(cot_rows)
    dual = split_groups(lat_apply(dual_lon, lat_fwd_table, lat_scale) * mode_weight)
    back = block_adjoint(dual, second_adj)
    pre = (back * gelu_slope(inner)).astype(jnp.bfloat16)
    back_spec = join_groups(block_adjoint(pre, first_adj))
    back_lon = lat_apply(back_spec, lat_inv_table, lat_scale)
    pull = to_cells(back_lon)
    layer_out = (cell_rows.astype(jnp.float32) + wave.astype(jnp.float32)).astype(jnp.bfloat16)
    field_grad = (cot_rows.astype(jnp.float32) + pull.astype(jnp.float32)).astype(jnp.bfloat16)
    sample_count = lax.axis_size("dp")
    second_term = block_outer(act, dual) / sample_count
    first_term = block_outer(spectrum, pre) / sample_count
    first_grad, second_grad = lax.psum((first_term, second_term), ("dp", "lon"))
    return (layer_out[None], field_grad[None], first_grad, second_grad)


def solution(mesh):
    placed = (P("dp", "lon", None, None), P("dp", "lon", None, None), P(), P())
    return jax.shard_map(
        on_device,
        mesh=mesh,
        in_specs=placed,
        out_specs=(P("dp", "lon", None, None), P("dp", "lon", None, None), P(), P()),
        check_vma=False,
    )
```

profile of v0, /device:TPU:1, one launch (start us, length us, event | category | flops | bytes accessed | tf_op | source)
XLA Modules:
  0.0 643.6 jit_solution(1187848861176454927)
XLA Ops:
  9.3 3.1 reshape.309
  12.4 11.0 %all-to-all-start = ((bf16[16,2,9216]{2,1,0:T(2,128)(2,1)}), bf16[16,2,9216]{2,1,0:T(2,128)(2,1)}, u32[]{:S(2)}, u32[]{:S(2)}) async-start(bf16[16,2,9216]{2,1,0:T(2,128)(2,1)} %reshape.309), calls=%async_computation | async-start | bytes 1179648 | tf_op jit(solution)/shard_map/all_to_all | solution.py:108
  24.6 3.1 reshape.317
  30.0 4.0 all-to-all-done
  34.1 5.2 all-to-all-start.4
  40.8 2.4 reshape.310
  47.2 3.1 reshape.311
  50.3 6.4 %all-to-all-start.1 = ((bf16[16,2,9216]{2,1,0:T(2,128)(2,1)}), bf16[16,2,9216]{2,1,0:T(2,128)(2,1)}, u32[]{:S(2)}, u32[]{:S(2)}) async-start(bf16[16,2,9216]{2,1,0:T(2,128)(2,1)} %reshape.311), calls=%async_computation.1 | async-start | bytes 1179648 | tf_op jit(solution)/shard_map/all_to_all | solution.py:101
  59.0 2.4 reshape.318
  65.4 3.1 reshape.319
  68.5 5.9 all-to-all-start.5
  77.1 2.4 reshape.312
  85.0 2.4 reshape.320
  89.7 2.9 reshape.288
  101.3 3.1 reshape.321
  104.4 4.5 all-to-all-start.6
  113.5 2.2 copy.132
  115.7 4.1 reshape.313
  121.4 5.8 all-to-all-start.2
  135.6 3.1 reshape.323
  138.7 5.7 all-to-all-start.7
  144.4 2.4 reshape.314
  151.4 3.1 reshape.315
  154.5 451.1 %all-reduce.3.cloned.1.call-done = (f32[2,8,96,96]{2,3,1,0:T(8,128)}, f32[2,8,96,96]{2,3,1,0:T(8,128)}) async-done(((f32[2,8,96,96]{2,3,1,0:T(8,128)}, f32[2,8,96,96]{2,3,1,0:T(8,128)}), (f32[2,8,96,96]{2,3,1,0:T(8,128)}, f32[2,8,96,96]{2,3,1,0:T(8,128)})) %all-reduce.3.cloned.1.call-update) | async-done | bytes 1179664 | tf_op jit(solution)/shard_map/psum | solution.py:141
  605.7 2.4 copy.158
  609.2 7.4 %all-to-all-start.3 = ((bf16[16,2,9216]{2,1,0:T(2,128)(2,1)}), bf16[16,2,9216]{2,1,0:T(2,128)(2,1)}, u32[]{:S(2)}, u32[]{:S(2)}) async-start(bf16[16,2,9216]{2,1,0:T(2,128)(2,1)} %reshape.315), calls=%async_computation.3 | async-start | bytes 1179648 | tf_op jit(solution)/shard_map/all_to_all | solution.py:104
  616.6 2.4 reshape.324
  621.2 2.2 reshape.269
  623.5 2.3 add_convert_fusion
  627.1 2.4 reshape.316
  631.7 2.2 reshape.268
  634.0 2.3 add_convert_fusion.1
  (139 shorter events, 61.8 us)
Async XLA Ops:
  12.3 11.0 %copy-start = (bf16[1,8,48,768]{3,2,1,0:T(8,128)(2,1)S(1)}, bf16[1,8,48,768]{3,2,1,0:T(8,128)(2,1)}, u32[]{:S(2)}) copy-start(bf16[1,8,48,768]{3,2,1,0:T(8,128)(2,1)} %param.5) | copy-start | bytes 1769476
  12.4 21.7 %all-to-all-start = ((bf16[16,2,9216]{2,1,0:T(2,128)(2,1)}), bf16[16,2,9216]{2,1,0:T(2,128)(2,1)}, u32[]{:S(2)}, u32[]{:S(2)}) async-start(bf16[16,2,9216]{2,1,0:T(2,128)(2,1)} %reshape.309), calls=%async_computation | async-start | bytes 1179648 | tf_op jit(solution)/shard_map/all_to_all | solution.py:108
  24.6 15.4 %copy-start.21 = (bf16[2,8,96,96]{3,2,1,0:T(8,128)(2,1)S(1)}, bf16[2,8,96,96]{3,2,1,0:T(8,128)(2,1)}, u32[]{:S(2)}) copy-start(bf16[2,8,96,96]{3,2,1,0:T(8,128)(2,1)} %param.6) | copy-start | bytes 884740
  34.1 16.2 %all-to-all-start.4 = ((bf16[16,2,9216]{2,1,0:T(2,128)(2,1)}), bf16[16,2,9216]{2,1,0:T(2,128)(2,1)}, u32[]{:S(2)}, u32[]{:S(2)}) async-start(bf16[16,2,9216]{2,1,0:T(2,128)(2,1)} %reshape.317), calls=%async_computation.4 | async-start | bytes 1179648 | tf_op jit(solution)/shard_map/all_to_all | solution.py:108
  47.2 9.6 %copy-start.29 = (bf16[48,1,48]{2,0,1:T(8,128)(2,1)S(1)}, bf16[48,1,48]{2,0,1:T(8,128)(2,1)}, u32[]{:S(2)}) copy-start(bf16[48,1,48]{2,0,1:T(8,128)(2,1)} %get-tuple-element.48) | copy-start | bytes 13828
  47.2 9.6 %copy-start.30 = (bf16[48,1,48]{2,0,1:T(8,128)(2,1)S(1)}, bf16[48,1,48]{2,0,1:T(8,128)(2,1)}, u32[]{:S(2)}) copy-start(bf16[48,1,48]{2,0,1:T(8,128)(2,1)} %get-tuple-element.49) | copy-start | bytes 13828
  47.2 9.6 %copy-start.31 = (bf16[48,1,48]{2,0,1:T(8,128)(2,1)S(1)}, bf16[48,1,48]{2,0,1:T(8,128)(2,1)}, u32[]{:S(2)}) copy-start(bf16[48,1,48]{2,0,1:T(8,128)(2,1)} %fusion.91) | copy-start | bytes 13828
  47.2 10.2 %copy-start.22 = (bf16[2,8,96,96]{3,2,1,0:T(8,128)(2,1)S(1)}, bf16[2,8,96,96]{3,2,1,0:T(8,128)(2,1)}, u32[]{:S(2)}) copy-start(bf16[2,8,96,96]{3,2,1,0:T(8,128)(2,1)} %param.7) | copy-start | bytes 884740
  50.3 18.2 %all-to-all-start.1 = ((bf16[16,2,9216]{2,1,0:T(2,128)(2,1)}), bf16[16,2,9216]{2,1,0:T(2,128)(2,1)}, u32[]{:S(2)}, u32[]{:S(2)}) async-start(bf16[16,2,9216]{2,1,0:T(2,128)(2,1)} %reshape.311), calls=%async_computation.1 | async-start | bytes 1179648 | tf_op jit(solution)/shard_map/all_to_all | solution.py:101
  65.4 9.5 %copy-start.8 = (bf16[1,8,96,96]{3,2,0,1:T(8,128)(2,1)S(1)}, bf16[1,8,96,96]{3,2,0,1:T(8,128)(2,1)}, u32[]{:S(2)}) copy-start(bf16[1,8,96,96]{3,2,0,1:T(8,128)(2,1)} %get-tuple-element.26) | copy-start | bytes 442372
  65.4 9.5 %copy-start.9 = (bf16[1,8,96,96]{3,2,0,1:T(8,128)(2,1)S(1)}, bf16[1,8,96,96]{3,2,0,1:T(8,128)(2,1)}, u32[]{:S(2)}) copy-start(bf16[1,8,96,96]{3,2,0,1:T(8,128)(2,1)} %get-tuple-element.27) | copy-start | bytes 442372
  65.4 9.5 %copy-start.10 = (bf16[1,8,96,96]{3,2,0,1:T(8,128)(2,1)S(1)}, bf16[1,8,96,96]{3,2,0,1:T(8,128)(2,1)}, u32[]{:S(2)}) copy-start(bf16[1,8,96,96]{3,2,0,1:T(8,128)(2,1)} %get-tuple-element.28) | copy-start | bytes 442372
  68.5 7.5 %copy-start.11 = (bf16[1,8,96,96]{3,2,0,1:T(8,128)(2,1)S(1)}, bf16[1,8,96,96]{3,2,0,1:T(8,128)(2,1)}, u32[]{:S(2)}) copy-start(bf16[1,8,96,96]{3,2,0,1:T(8,128)(2,1)} %get-tuple-element.31) | copy-start | bytes 442372
  68.5 7.5 %copy-start.12 = (bf16[1,8,96,96]{3,2,0,1:T(8,128)(2,1)S(1)}, bf16[1,8,96,96]{3,2,0,1:T(8,128)(2,1)}, u32[]{:S(2)}) copy-start(bf16[1,8,96,96]{3,2,0,1:T(8,128)(2,1)} %get-tuple-element.32) | copy-start | bytes 442372
  68.5 7.5 %copy-start.13 = (bf16[1,8,96,96]{3,2,0,1:T(8,128)(2,1)S(1)}, bf16[1,8,96,96]{3,2,0,1:T(8,128)(2,1)}, u32[]{:S(2)}) copy-start(bf16[1,8,96,96]{3,2,0,1:T(8,128)(2,1)} %get-tuple-element.33) | copy-start | bytes 442372
  68.5 16.5 %all-to-all-start.5 = ((bf16[16,2,9216]{2,1,0:T(2,128)(2,1)}), bf16[16,2,9216]{2,1,0:T(2,128)(2,1)}, u32[]{:S(2)}, u32[]{:S(2)}) async-start(bf16[16,2,9216]{2,1,0:T(2,128)(2,1)} %reshape.319), calls=%async_computation.5 | async-start | bytes 1179648 | tf_op jit(solution)/shard_map/all_to_all | solution.py:101
  80.6 1.6 copy-start.25
  80.6 1.6 copy-start.27
  89.7 2.9 copy-start.26
  89.7 2.9 copy-start.28
  89.7 2.9 copy-start.32
  94.8 1.7 copy-start.7
  94.8 1.7 copy-start.19
  94.8 1.6 copy-start.20
  96.5 1.3 copy-start.18
  101.3 7.6 %copy-start.3 = (bf16[2,8,96,96]{3,2,0,1:T(8,128)(2,1)S(1)}, bf16[2,8,96,96]{3,2,0,1:T(8,128)(2,1)}, u32[]{:S(2)}) copy-start(bf16[2,8,96,96]{3,2,0,1:T(8,128)(2,1)} %copy-done.2) | copy-start | bytes 884740
  104.4 17.0 %all-to-all-start.6 = ((bf16[16,2,9216]{2,1,0:T(2,128)(2,1)}), bf16[16,2,9216]{2,1,0:T(2,128)(2,1)S(1)}, u32[]{:S(2)}, u32[]{:S(2)}) async-start(bf16[16,2,9216]{2,1,0:T(2,128)(2,1)} %reshape.321), calls=%async_computation.6 | async-start | bytes 1179648 | tf_op jit(solution)/shard_map/all_to_all | solution.py:113
  121.4 17.3 %all-to-all-start.2 = ((bf16[16,2,9216]{2,1,0:T(2,128)(2,1)}), bf16[16,2,9216]{2,1,0:T(2,128)(2,1)}, u32[]{:S(2)}, u32[]{:S(2)}) async-start(bf16[16,2,9216]{2,1,0:T(2,128)(2,1)} %reshape.313), calls=%async_computation.2 | async-start | bytes 1179648 | tf_op jit(solution)/shard_map/all_to_all | solution.py:113
  127.2 478.5 %all-reduce.3.cloned.1.call-start = ((), (), s32[]{:S(2)}) async-start(), calls=%async_computation.8 | async-start | bytes 3145728 | tf_op jit(solution)/shard_map/psum | solution.py:141
  138.7 470.5 %all-to-all-start.7 = ((bf16[16,2,9216]{2,1,0:T(2,128)(2,1)}), bf16[16,2,9216]{2,1,0:T(2,128)(2,1)}, u32[]{:S(2)}, u32[]{:S(2)}) async-start(bf16[16,2,9216]{2,1,0:T(2,128)(2,1)} %reshape.323), calls=%async_computation.7 | async-start | bytes 1179648 | tf_op jit(solution)/shard_map/all_to_all | solution.py:104
  605.7 2.4 copy-start.4
  609.2 17.9 %all-to-all-start.3 = ((bf16[16,2,9216]{2,1,0:T(2,128)(2,1)}), bf16[16,2,9216]{2,1,0:T(2,128)(2,1)}, u32[]{:S(2)}, u32[]{:S(2)}) async-start(bf16[16,2,9216]{2,1,0:T(2,128)(2,1)} %reshape.315), calls=%async_computation.3 | async-start | bytes 1179648 | tf_op jit(solution)/shard_map/all_to_all | solution.py:104
  (10 other events, 11.0 us)
Sparse Core Ops, SparseCore 0:
  133.9 471.6 all-reduce.2
where the time goes:
time: 652 us; the launch traced here: 644 us
  waiting for transfers between devices  458 us (70%)
  local copies, waits for them, and re-layouts  88.6 us (14%)
  starting transfers between devices  52 us (8%)
  other arithmetic  17.4 us (3%)
  between operations  15.2 us (2%)
  matrix products  12.2 us (2%)
    psum x1, waiting for transfers between devices, on_device(): first_grad, second_grad = lax.psum((first_term, second_term), ('dp', 'lon'))  451 us
    unnamed x90, local copies, waits for them, and re-layouts  52.7 us
    all_to_all x2, starting transfers between devices, to_spectrum(): lax.all_to_all(grid_rows, 'lon', split_axis=2, concat_axis=0, tiled=True)  16.1 us
    all_to_all x2, starting transfers between devices, modes_to_lines(): lax.all_to_all(local_idft(all_modes), 'lon', split_axis=0, concat_axis=2,...  13.2 us
  transfers between devices with their start and end apart: 9, of which 4 were waited for; matrix products, arithmetic and copies ran while one was open for 13% of the time, Pallas kernels for 0%

commit v1 on v0

--- a/solution.py
+++ b/solution.py
@@ -138,7 +138,15 @@
     sample_count = lax.axis_size("dp")
     second_term = block_outer(act, dual) / sample_count
     first_term = block_outer(spectrum, pre) / sample_count
-    first_grad, second_grad = lax.psum((first_term, second_term), ("dp", "lon"))
+
+    def process_series_all(mat):
+        mesh_dim = "dp"
+        bus_axis = "lon"
+        for k in (bus_axis, mesh_dim):
+            mat = lax.psum(mat, axis_name=k)
+        return mat
+
+    first_grad, second_grad = process_series_all((first_term, second_term))
     return (layer_out[None], field_grad[None], first_grad, second_grad)
 
 

time: 652 us -> 612 us (0.939)
  the two profiles are of different devices: /device:TPU:1 before, /device:TPU:8 now
where the time goes in v1:
time: 612 us; the launch traced here: 604 us
  waiting for transfers between devices  412 us (67%)
  local copies, waits for them, and re-layouts  89.6 us (15%)
  starting transfers between devices  54.3 us (9%)
  other arithmetic  17.8 us (3%)
  between operations  15.3 us (2%)
  matrix products  14.4 us (2%)
    psum x2, waiting for transfers between devices, process_series_all(): mat = lax.psum(mat, axis_name=k)  408 us
    unnamed x98, local copies, waits for them, and re-layouts  52 us
    all_to_all x2, starting transfers between devices, to_spectrum(): lax.all_to_all(grid_rows, 'lon', split_axis=2, concat_axis=0, tiled=True)  16.8 us
    all_to_all x2, starting transfers between devices, to_cells(): lax.all_to_all(spec_rows, 'lon', split_axis=3, concat_axis=0, tiled=True)  12.5 us
    all_to_all x2, starting transfers between devices, lines_to_modes(): lax.all_to_all(local_dft(all_lines), 'lon', split_axis=0, concat_axis=3,...  12.3 us
  transfers between devices with their start and end apart: 10, of which 5 were waited for; matrix products, arithmetic and copies ran while one was open for 15% of the time, Pallas kernels for 0%

profile of v1, /device:TPU:8, one launch (start us, length us, event | category | flops | bytes accessed | tf_op | source)
XLA Modules:
  0.0 603.5 jit_solution(5722045798979228778)
XLA Ops:
  9.3 3.1 reshape.309
  12.4 10.0 %all-to-all-start = ((bf16[16,2,9216]{2,1,0:T(2,128)(2,1)}), bf16[16,2,9216]{2,1,0:T(2,128)(2,1)}, u32[]{:S(2)}, u32[]{:S(2)}) async-start(bf16[16,2,9216]{2,1,0:T(2,128)(2,1)} %reshape.309), calls=%async_computation | async-start | bytes 1179648 | tf_op jit(solution)/shard_map/all_to_all | solution.py:108
  23.5 3.1 reshape.317
  29.0 2.4 all-to-all-done
  31.4 6.8 %all-to-all-start.4 = ((bf16[16,2,9216]{2,1,0:T(2,128)(2,1)}), bf16[16,2,9216]{2,1,0:T(2,128)(2,1)}, u32[]{:S(2)}, u32[]{:S(2)}) async-start(bf16[16,2,9216]{2,1,0:T(2,128)(2,1)} %reshape.317), calls=%async_computation.4 | async-start | bytes 1179648 | tf_op jit(solution)/shard_map/all_to_all | solution.py:108
  39.8 2.4 reshape.310
  46.2 3.1 reshape.311
  49.3 6.4 %all-to-all-start.1 = ((bf16[16,2,9216]{2,1,0:T(2,128)(2,1)}), bf16[16,2,9216]{2,1,0:T(2,128)(2,1)}, u32[]{:S(2)}, u32[]{:S(2)}) async-start(bf16[16,2,9216]{2,1,0:T(2,128)(2,1)} %reshape.311), calls=%async_computation.1 | async-start | bytes 1179648 | tf_op jit(solution)/shard_map/all_to_all | solution.py:101
  58.0 2.4 reshape.318
  64.4 3.1 reshape.319
  67.5 5.9 all-to-all-start.5
  76.0 2.4 reshape.312
  82.4 2.4 reshape.320
  87.1 2.9 reshape.288
  98.5 2.5 copy.148
  101.0 3.1 reshape.321
  104.1 6.7 %all-to-all-start.6 = ((bf16[16,2,9216]{2,1,0:T(2,128)(2,1)}), bf16[16,2,9216]{2,1,0:T(2,128)(2,1)}, u32[]{:S(2)}, u32[]{:S(2)}) async-start(bf16[16,2,9216]{2,1,0:T(2,128)(2,1)} %reshape.321), calls=%async_computation.6 | async-start | bytes 1179648 | tf_op jit(solution)/shard_map/all_to_all | solution.py:113
  115.0 3.0 convolution_bitcast_fusion
  118.0 2.5 copy.132
  120.5 3.1 reshape.313
  125.2 5.8 all-to-all-start.2
  133.2 2.4 reshape.322
  140.2 3.1 reshape.323
  143.3 5.7 all-to-all-start.7
  149.1 2.4 reshape.314
  156.1 3.1 reshape.315
  160.8 6.5 %all-to-all-start.3 = ((bf16[16,2,9216]{2,1,0:T(2,128)(2,1)}), bf16[16,2,9216]{2,1,0:T(2,128)(2,1)}, u32[]{:S(2)}, u32[]{:S(2)}) async-start(bf16[16,2,9216]{2,1,0:T(2,128)(2,1)} %reshape.315), calls=%async_computation.3 | async-start | bytes 1179648 | tf_op jit(solution)/shard_map/all_to_all | solution.py:104
  167.6 2.5 reshape.324
  170.0 101.2 %all-reduce.7.cloned.1.call-done = (f32[2,8,96,96]{2,3,1,0:T(8,128)}, f32[2,8,96,96]{2,3,1,0:T(8,128)}) async-done(((f32[2,8,96,96]{2,3,1,0:T(8,128)}, f32[2,8,96,96]{2,3,1,0:T(8,128)}), (f32[2,8,96,96]{2,3,1,0:T(8,128)}, f32[2,8,96,96]{2,3,1,0:T(8,128)})) %all-reduce.7.cloned.1.call-update) | async-done | bytes 1179664 | tf_op jit(solution)/shard_map/psum | solution.py:146
  275.6 2.4 reshape.316
  282.5 2.5 add_convert_fusion
  285.9 306.9 %all-reduce.5.cloned.1.call-done = (f32[2,8,96,96]{2,3,1,0:T(8,128)}, f32[2,8,96,96]{2,3,1,0:T(8,128)}) async-done(((f32[2,8,96,96]{2,3,1,0:T(8,128)}, f32[2,8,96,96]{2,3,1,0:T(8,128)}), (f32[2,8,96,96]{2,3,1,0:T(8,128)}, f32[2,8,96,96]{2,3,1,0:T(8,128)})) %all-reduce.5.cloned.1.call-update) | async-done | bytes 1179664 | tf_op jit(solution)/shard_map/psum | solution.py:146
  (150 shorter events, 66.4 us)
Async XLA Ops:
  12.3 10.0 %copy-start.1 = (bf16[1,8,48,768]{3,2,1,0:T(8,128)(2,1)S(1)}, bf16[1,8,48,768]{3,2,1,0:T(8,128)(2,1)}, u32[]{:S(2)}) copy-start(bf16[1,8,48,768]{3,2,1,0:T(8,128)(2,1)} %param.5) | copy-start | bytes 1769476
  12.4 19.0 %all-to-all-start = ((bf16[16,2,9216]{2,1,0:T(2,128)(2,1)}), bf16[16,2,9216]{2,1,0:T(2,128)(2,1)}, u32[]{:S(2)}, u32[]{:S(2)}) async-start(bf16[16,2,9216]{2,1,0:T(2,128)(2,1)} %reshape.309), calls=%async_computation | async-start | bytes 1179648 | tf_op jit(solution)/shard_map/all_to_all | solution.py:108
  23.5 15.4 %copy-start.22 = (bf16[2,8,96,96]{3,2,1,0:T(8,128)(2,1)S(1)}, bf16[2,8,96,96]{3,2,1,0:T(8,128)(2,1)}, u32[]{:S(2)}) copy-start(bf16[2,8,96,96]{3,2,1,0:T(8,128)(2,1)} %param.6) | copy-start | bytes 884740
  31.4 17.9 %all-to-all-start.4 = ((bf16[16,2,9216]{2,1,0:T(2,128)(2,1)}), bf16[16,2,9216]{2,1,0:T(2,128)(2,1)}, u32[]{:S(2)}, u32[]{:S(2)}) async-start(bf16[16,2,9216]{2,1,0:T(2,128)(2,1)} %reshape.317), calls=%async_computation.4 | async-start | bytes 1179648 | tf_op jit(solution)/shard_map/all_to_all | solution.py:108
  46.1 9.6 %copy-start.32 = (bf16[48,1,48]{2,0,1:T(8,128)(2,1)S(1)}, bf16[48,1,48]{2,0,1:T(8,128)(2,1)}, u32[]{:S(2)}) copy-start(bf16[48,1,48]{2,0,1:T(8,128)(2,1)} %get-tuple-element.50) | copy-start | bytes 13828
  46.1 9.6 %copy-start.33 = (bf16[48,1,48]{2,0,1:T(8,128)(2,1)S(1)}, bf16[48,1,48]{2,0,1:T(8,128)(2,1)}, u32[]{:S(2)}) copy-start(bf16[48,1,48]{2,0,1:T(8,128)(2,1)} %get-tuple-element.51) | copy-start | bytes 13828
  46.2 9.6 %copy-start.34 = (bf16[48,1,48]{2,0,1:T(8,128)(2,1)S(1)}, bf16[48,1,48]{2,0,1:T(8,128)(2,1)}, u32[]{:S(2)}) copy-start(bf16[48,1,48]{2,0,1:T(8,128)(2,1)} %fusion.91) | copy-start | bytes 13828
  46.2 10.2 %copy-start.23 = (bf16[2,8,96,96]{3,2,1,0:T(8,128)(2,1)S(1)}, bf16[2,8,96,96]{3,2,1,0:T(8,128)(2,1)}, u32[]{:S(2)}) copy-start(bf16[2,8,96,96]{3,2,1,0:T(8,128)(2,1)} %param.7) | copy-start | bytes 884740
  49.3 18.2 %all-to-all-start.1 = ((bf16[16,2,9216]{2,1,0:T(2,128)(2,1)}), bf16[16,2,9216]{2,1,0:T(2,128)(2,1)}, u32[]{:S(2)}, u32[]{:S(2)}) async-start(bf16[16,2,9216]{2,1,0:T(2,128)(2,1)} %reshape.311), calls=%async_computation.1 | async-start | bytes 1179648 | tf_op jit(solution)/shard_map/all_to_all | solution.py:101
  64.3 9.5 %copy-start.9 = (bf16[1,8,96,96]{3,2,0,1:T(8,128)(2,1)S(1)}, bf16[1,8,96,96]{3,2,0,1:T(8,128)(2,1)}, u32[]{:S(2)}) copy-start(bf16[1,8,96,96]{3,2,0,1:T(8,128)(2,1)} %get-tuple-element.28) | copy-start | bytes 442372
  64.3 9.5 %copy-start.10 = (bf16[1,8,96,96]{3,2,0,1:T(8,128)(2,1)S(1)}, bf16[1,8,96,96]{3,2,0,1:T(8,128)(2,1)}, u32[]{:S(2)}) copy-start(bf16[1,8,96,96]{3,2,0,1:T(8,128)(2,1)} %get-tuple-element.29) | copy-start | bytes 442372
  64.3 9.5 %copy-start.11 = (bf16[1,8,96,96]{3,2,0,1:T(8,128)(2,1)S(1)}, bf16[1,8,96,96]{3,2,0,1:T(8,128)(2,1)}, u32[]{:S(2)}) copy-start(bf16[1,8,96,96]{3,2,0,1:T(8,128)(2,1)} %get-tuple-element.30) | copy-start | bytes 442372
  67.4 7.5 %copy-start.12 = (bf16[1,8,96,96]{3,2,0,1:T(8,128)(2,1)S(1)}, bf16[1,8,96,96]{3,2,0,1:T(8,128)(2,1)}, u32[]{:S(2)}) copy-start(bf16[1,8,96,96]{3,2,0,1:T(8,128)(2,1)} %get-tuple-element.33) | copy-start | bytes 442372
  67.4 7.5 %copy-start.13 = (bf16[1,8,96,96]{3,2,0,1:T(8,128)(2,1)S(1)}, bf16[1,8,96,96]{3,2,0,1:T(8,128)(2,1)}, u32[]{:S(2)}) copy-start(bf16[1,8,96,96]{3,2,0,1:T(8,128)(2,1)} %get-tuple-element.34) | copy-start | bytes 442372
  67.4 7.5 %copy-start.14 = (bf16[1,8,96,96]{3,2,0,1:T(8,128)(2,1)S(1)}, bf16[1,8,96,96]{3,2,0,1:T(8,128)(2,1)}, u32[]{:S(2)}) copy-start(bf16[1,8,96,96]{3,2,0,1:T(8,128)(2,1)} %get-tuple-element.35) | copy-start | bytes 442372
  67.5 15.0 %all-to-all-start.5 = ((bf16[16,2,9216]{2,1,0:T(2,128)(2,1)}), bf16[16,2,9216]{2,1,0:T(2,128)(2,1)}, u32[]{:S(2)}, u32[]{:S(2)}) async-start(bf16[16,2,9216]{2,1,0:T(2,128)(2,1)} %reshape.319), calls=%async_computation.5 | async-start | bytes 1179648 | tf_op jit(solution)/shard_map/all_to_all | solution.py:101
  79.5 1.6 copy-start.28
  87.1 2.9 copy-start.29
  87.1 2.9 copy-start.31
  87.1 2.9 copy-start.35
  91.2 1.9 copy-start.8
  101.0 9.8 %copy-start.5 = (bf16[2,8,96,96]{3,2,0,1:T(8,128)(2,1)S(1)}, bf16[2,8,96,96]{3,2,0,1:T(8,128)(2,1)}, u32[]{:S(2)}) copy-start(bf16[2,8,96,96]{3,2,0,1:T(8,128)(2,1)} %copy-done.4) | copy-start | bytes 884740
  104.1 21.1 %all-to-all-start.6 = ((bf16[16,2,9216]{2,1,0:T(2,128)(2,1)}), bf16[16,2,9216]{2,1,0:T(2,128)(2,1)}, u32[]{:S(2)}, u32[]{:S(2)}) async-start(bf16[16,2,9216]{2,1,0:T(2,128)(2,1)} %reshape.321), calls=%async_computation.6 | async-start | bytes 1179648 | tf_op jit(solution)/shard_map/all_to_all | solution.py:113
  123.7 7.5 %copy-start.6 = (f32[1,8,96,96]{2,3,1,0:T(8,128)S(1)}, f32[1,8,96,96]{2,3,1,0:T(8,128)}, u32[]{:S(2)}) copy-start(f32[1,8,96,96]{2,3,1,0:T(8,128)} %fusion.70) | copy-start | bytes 884740
  125.2 18.1 %all-to-all-start.2 = ((bf16[16,2,9216]{2,1,0:T(2,128)(2,1)}), bf16[16,2,9216]{2,1,0:T(2,128)(2,1)}, u32[]{:S(2)}, u32[]{:S(2)}) async-start(bf16[16,2,9216]{2,1,0:T(2,128)(2,1)} %reshape.313), calls=%async_computation.2 | async-start | bytes 1179648 | tf_op jit(solution)/shard_map/all_to_all | solution.py:113
  131.0 140.3 %all-reduce.7.cloned.1.call-start = ((), (), s32[]{:S(2)}) async-start(), calls=%async_computation.9 | async-start | bytes 3145728 | tf_op jit(solution)/shard_map/psum | solution.py:146
  143.3 17.4 %all-to-all-start.7 = ((bf16[16,2,9216]{2,1,0:T(2,128)(2,1)}), bf16[16,2,9216]{2,1,0:T(2,128)(2,1)}, u32[]{:S(2)}, u32[]{:S(2)}) async-start(bf16[16,2,9216]{2,1,0:T(2,128)(2,1)} %reshape.323), calls=%async_computation.7 | async-start | bytes 1179648 | tf_op jit(solution)/shard_map/all_to_all | solution.py:104
  160.8 114.9 %all-to-all-start.3 = ((bf16[16,2,9216]{2,1,0:T(2,128)(2,1)}), bf16[16,2,9216]{2,1,0:T(2,128)(2,1)}, u32[]{:S(2)}, u32[]{:S(2)}) async-start(bf16[16,2,9216]{2,1,0:T(2,128)(2,1)} %reshape.315), calls=%async_computation.3 | async-start | bytes 1179648 | tf_op jit(solution)/shard_map/all_to_all | solution.py:104
  167.3 425.5 %all-reduce.5.cloned.1.call-start = ((), (), s32[]{:S(2)}) async-start(), calls=%async_computation.8 | async-start | bytes 3145728 | tf_op jit(solution)/shard_map/psum | solution.py:146
  282.5 2.5 copy-start
  282.5 2.5 copy-start.2
  592.7 2.4 copy-start.7
  (15 other events, 18.1 us)
Sparse Core Ops, SparseCore 0:
  135.3 135.8 all-reduce.6
  274.4 318.2 all-reduce.4
